TPU v7x, 32 devices: a whole 2x2x4 slice. The times are simulated.
32 devices in a mesh: groups: 2 (over x), dp: 16 (over z, y, core).
Axes of the slice: x: 2, y: 2, z: 4, core: 2. Of those that a mesh axis runs over, the one named last changes fastest.
Arguments:
- tokens: bfloat16 [12288, 8192], P(('groups', 'dp')), parts along dimension 0, may hold values from -6 to 6
- base_weight: bfloat16 [8192, 768], P('dp'), may hold values from -0.0625 to 0.0625
- down_stack: bfloat16 [8192, 512], P('dp'), may hold values from -0.0625 to 0.0625
- up_stack: bfloat16 [512, 768], replicated, may hold values from -0.75 to 0.75
- adapter_scale: float32 [8], replicated, may hold values from 0.5 to 2
- lengths: int32 [64], P(('groups', 'dp')), parts along dimension 0, may hold values from 1 to 256, as said below
- adapter_ids: int32 [64], P(('groups', 'dp')), parts along dimension 0, may hold values from 0 to 7
Outputs:
- projected: bfloat16 [12288, 768], P(('groups', 'dp')), parts along dimension 0
There are 2 independent parts, one for each index of `groups`. A program takes and returns all parts, laid end to end along the dimension named above; an argument that names none is the same for every part. Nothing has to cross between parts.
Inputs may be any that keep to these rules, and one draw needn't show every extreme that they name: `lengths`: each index of dp holds two requests whose block counts ceil(length / 128) add up to exactly 3.
All inputs are finite; a program needn't handle non-finite values.
Results may differ from a plain program's by a relative error of at most 0.0042.
Values may be sent and summed in bfloat16 or wider, within the bound.
A program may use at most 128 MiB of HBM per device.

v0:
```python
import jax
import jax.numpy as jnp
from jax import lax
from jax.sharding import PartitionSpec as P

RANK = 64
BLOCK = 128


def layout(lengths, adapter_ids, row_count):
    counts = (lengths + BLOCK - 1) // BLOCK
    position = jnp.arange(row_count, dtype=jnp.int32)
    boundary = counts[0] * BLOCK
    second = position >= boundary
    offset = jnp.where(second, position - boundary, position)
    is_live = offset < jnp.where(second, lengths[1], lengths[0])
    token_adapter = jnp.where(second, adapter_ids[1], adapter_ids[0])
    return (is_live, token_adapter)


def local(tokens, base_weight, down_stack, up_stack, adapter_scale, lengths, adapter_ids):
    row_count = tokens.shape[0]
    num_blocks = row_count // BLOCK
    adapters = down_stack.shape[1] // RANK
    is_live, token_adapter = layout(lengths, adapter_ids, row_count)
    adapter_per_block = token_adapter.reshape(num_blocks, BLOCK)[:, 0]
    w_piece = lax.all_gather(base_weight, "dp", axis=0, tiled=True)
    a_piece = lax.all_gather(down_stack, "dp", axis=0, tiled=True)
    width_dev = w_piece.shape[0]
    base_projection_share = jnp.dot(tokens, w_piece, preferred_element_type=jnp.float32)
    down_split = a_piece.reshape(width_dev, adapters, RANK)
    selected_adapter = jnp.take(down_split, adapter_per_block, axis=1)
    token_block_groups = tokens.reshape(num_blocks, BLOCK, width_dev)
    low_part = jnp.einsum(
        "wmu,uwi->wmi", token_block_groups, selected_adapter, preferred_element_type=jnp.float32
    )
    low_rank = low_part.reshape(row_count, RANK)
    low_rank = low_rank.astype(jnp.bfloat16)
    onehot = token_adapter[:, None] == jnp.arange(adapters, dtype=jnp.int32)[None, :]
    widened = jnp.where(
        onehot[:, :, None], low_rank[:, None, :], jnp.zeros((), jnp.bfloat16)
    ).reshape(row_count, adapters * RANK)
    adapter_out = jnp.dot(widened, up_stack, preferred_element_type=jnp.float32)
    token_scale = jnp.sum(jnp.where(onehot, adapter_scale[None, :], 0.0), axis=1)
    result = jnp.where(
        is_live[:, None], base_projection_share + token_scale[:, None] * adapter_out, 0.0
    )
    return result.astype(jnp.bfloat16)


def solution(mesh):
    in_specs = (
        P(("groups", "dp"), None),
        P("dp", None),
        P("dp", None),
        P(),
        P(),
        P(("groups", "dp")),
        P(("groups", "dp")),
    )
    out_specs = P(("groups", "dp"), None)
    return jax.shard_map(local, mesh=mesh, in_specs=in_specs, out_specs=out_specs, check_vma=False)
```

profile of v0, /device:TPU:0, one launch (start us, length us, event | category | flops | bytes accessed | tf_op | source)
XLA Modules:
  0.0 209.0 jit_solution(384807473434805781)
XLA Ops:
  6.5 0.0 copy-start
  6.5 0.0 all-gather.5.cloned.1.call-start
  6.5 2.1 %copy.8 = bf16[512,512]{0,1:T(8,128)(2,1)} copy(bf16[512,512]{1,0:T(8,128)(2,1)} %param.9) | data formatting | bytes 1048576 | tf_op args[2]
  8.7 0.0 all-gather.5.cloned.1.call-update
  8.7 0.0 all-gather.3.cloned.1.call-start
  8.7 0.7 all-gather.3.cloned.1.call-update
  9.4 0.7 and_select_fusion
  10.1 1.3 fusion.18
  11.5 1.2 and_bitcast_fusion
  12.7 1.2 fusion.16
  14.0 1.4 fusion.17
  15.3 1.2 select_compare_fusion
  16.6 1.2 fusion.14
  17.8 0.7 select_reduce_fusion
  18.6 71.4 %all-gather.5.cloned.1.call-done = bf16[8192,512]{0,1:T(8,128)(2,1)} async-done(((bf16[512,512]{0,1:T(8,128)(2,1)}), bf16[8192,512]{0,1:T(8,128)(2,1)}) %all-gather.5.cloned.1.call-update) | async-done | bytes 8388624 | tf_op jit(solution)/shard_map/all_gather | solution.py:28
  90.0 5.9 %gather_fusion = bf16[3,8192,64]{1,2,0:T(8,128)(2,1)} fusion(bf16[8192,8,64]{0,2,1:T(8,128)(2,1)} %bitcast.31, s32[1024]{0:T(1024)S(1)} %pad_clamp_fusion), kind=kCustom, calls=%fused_computation | custom fusion | bytes 6291468 | tf_op jit(solution)/shard_map/jit(_take)/gather | solution.py:32
  95.9 6.7 %fusion.11 = bf16[3,8,8,128]{3,2,1,0:T(8,128)(2,1)S(1)} fusion(bf16[3,128,8192]{2,1,0:T(8,128)(2,1)} %bitcast.34, bf16[3,8192,64]{1,2,0:T(8,128)(2,1)} %gather_fusion, pred[3]{0:T(512)(128)(4,1)S(1)} %and_bitcast_fusion), kind=kOutput, calls=%fused_computation.11 | convolution fusion | flops 404250624 | bytes 9486339 | tf_op jit(solution)/shard_map/wmu,uwi->wmi/dot_general | solution.py:34
  102.5 0.1 broadcast_select_fusion
  102.6 88.3 %all-gather.3.cloned.1.call-done = bf16[8192,768]{1,0:T(8,128)(2,1)} async-done(((bf16[512,768]{1,0:T(8,128)(2,1)}), bf16[8192,768]{1,0:T(8,128)(2,1)}) %all-gather.3.cloned.1.call-update) | async-done | bytes 12582928 | tf_op jit(solution)/shard_map/all_gather | solution.py:27
  190.9 9.9 %fusion.19 = f32[384,768]{1,0:T(8,128)S(1)} fusion(bf16[384,8192]{1,0:T(8,128)(2,1)} %param.7, bf16[8192,768]{1,0:T(8,128)(2,1)} %all-gather.3.cloned.1.call-done), kind=kOutput, calls=%fused_computation.33 | convolution fusion | flops 4831838208 | bytes 20054016 | tf_op jit(solution)/shard_map/dot_general | solution.py:30
  200.8 0.0 copy-done
  200.8 1.3 fusion.7
  (3 shorter events, 0.0 us)
Async XLA Ops:
  6.5 194.3 %copy-start = (bf16[512,768]{1,0:T(8,128)(2,1)S(1)}, bf16[512,768]{1,0:T(8,128)(2,1)}, u32[]{:S(2)}) copy-start(bf16[512,768]{1,0:T(8,128)(2,1)} %param.10) | copy-start | bytes 2359300
  6.5 83.4 %all-gather.5.cloned.1.call-start = ((), (), s32[]{:S(2)}) async-start(), calls=%async_computation.1 | async-start | bytes 8912896 | tf_op jit(solution)/shard_map/all_gather | solution.py:28
  8.7 182.2 %all-gather.3.cloned.1.call-start = ((), (), s32[]{:S(2)}) async-start(), calls=%async_computation | async-start | bytes 13369344 | tf_op jit(solution)/shard_map/all_gather | solution.py:27
Sparse Core Ops, SparseCore 0:
  9.5 80.4 all-gather.4
  92.2 98.5 all-gather.2
where the time goes:
time: 209 us
  waiting for transfers between devices  160 us (77%)
  matrix products  17.9 us (9%)
  between operations  13.5 us (6%)
  local copies, waits for them, and re-layouts  10.8 us (5%)
  other arithmetic  6.4 us (3%)
    all_gather x1, waiting for transfers between devices, local(): w_piece = lax.all_gather(base_weight, 'dp', axis=0, tiled=True)  88.3 us
    all_gather x1, waiting for transfers between devices, local(): a_piece = lax.all_gather(down_stack, 'dp', axis=0, tiled=True)  71.4 us
    dot_general x1, matrix products, local(): jnp.dot(tokens, w_piece, preferred_element_type=jnp.float32)  9.92 us
    dot_general x1, matrix products, local(): jnp.einsum('wmu,uwi->wmi', token_block_groups, selected_adapter, preferre...  6.65 us
    gather x1, local copies, waits for them, and re-layouts, local(): selected_adapter = jnp.take(down_split, adapter_per_block, axis=1)  5.9 us
  transfers between devices with their start and end apart: 2, of which 2 were waited for; matrix products, arithmetic and copies ran while one was open for 10% of the time, Pallas kernels for 0%

commit v1 on v0

v1 whole, which is shorter than its diff:
```python
import functools

import jax
import jax.numpy as jnp
from jax import lax
from jax.experimental import pallas as pl
from jax.experimental.pallas import tpu as pltpu
from jax.sharding import PartitionSpec as P

BLOCK = 128
PIECE = 32
MESH = pl.DeviceIdType.MESH


def plan(depth, pieces, special, first):
    gathered = pieces - special
    queues = {
        (z, d): []
        for z in range(depth)
        for d in "udyx"
        if not (d == "u" and z == depth - 1) and not (d == "d" and z == 0)
    }

    def targets(piece, via):
        if via == "x":
            return ""
        if piece in first:
            out = {"own": "udy", "y": "ud", "u": "u", "d": "d"}[via]
        else:
            out = {"own": "udy", "y": "", "u": "uy", "d": "dy"}[via]
        return out + "x" if piece < special and via != "own" else out

    own = [targets(k, "own") for k in range(gathered)]
    for z in range(depth):
        for k in range(gathered):
            for d in own[k]:
                if (z, d) in queues:
                    queues[z, d].append((z, 1, k))
    events = [[] for _ in range(depth)]
    while any(queues.values()):
        moved = [(z, d, q.pop(0)) for (z, d), q in queues.items() if q]
        for z, d, (owner, same, k) in sorted(moved, key=lambda m: "udyx".index(m[1])):
            at = z + (d == "u") - (d == "d")
            if d == "y":
                same = 1 - same
            out = "".join(o for o in targets(k, d) if (at, o) in queues)
            for o in out:
                queues[at, o].append((owner, same, k))
            events[at].append((d, owner, same, k, out))
    return events


def kernel(
    sizes, tok_hbm, base_hbm, down_hbm, up_hbm, scale_ref, len_ref, ids_ref, out_ref,
    held, tok, up, acc, load_sem, recv_sem, send_sem, own_sem, core_recv, core_send,
):
    depth, special, first, swap = sizes
    rows, base_cols = base_hbm.shape
    pieces = rows // PIECE
    gathered = pieces - special
    events = plan(depth, pieces, special, first)
    group, me = lax.axis_index("groups"), lax.axis_index("dp")
    core, y, z = me % 2, (me // 2) % 2, me // 4
    side = group % 2
    at = [z == k for k in range(depth)]

    def pick(values):
        if len(set(values)) == 1:
            return values[0]
        out = jnp.int32(values[0])
        for k in range(1, depth):
            if values[k] != values[0]:
                out = jnp.where(at[k], jnp.int32(values[k]), out)
        return out

    def when(flags, fn):
        if all(flags):
            fn()
        elif any(flags):
            pl.when(pick([int(f) for f in flags]) == 1)(fn)

    peers = {
        "u": (group, me + 4),
        "d": (group, me - 4),
        "y": (group, me + 2 - 4 * y),
        "x": (group + 1 - 2 * side, me),
        "p": (group, me + 1 - 2 * core),
    }
    has = {
        "u": [k < depth - 1 for k in range(depth)],
        "d": [k > 0 for k in range(depth)],
        "y": [True] * depth,
        "x": [swap] * depth,
        "p": [True] * depth,
    }
    kinds = "udyx"

    pair = z * 2 + y
    mine = pl.multiple_of(me * rows, rows)
    loads = [
        pltpu.make_async_copy(base_hbm, held.at[pl.ds(mine, rows), pl.ds(0, base_cols)], load_sem.at[0]),
        pltpu.make_async_copy(
            down_hbm, held.at[pl.ds(mine, rows), pl.ds(base_cols, down_hbm.shape[1])], load_sem.at[1]
        ),
        pltpu.make_async_copy(tok_hbm, tok, load_sem.at[2]),
        pltpu.make_async_copy(up_hbm, up, load_sem.at[3]),
    ]
    for load in loads:
        load.start()

    barrier = pltpu.get_barrier_semaphore()
    for d in "udyxp":
        def greet(d=d):
            pl.semaphore_signal(barrier, inc=1, device_id=peers[d], device_id_type=MESH)
        when(has[d], greet)
    pl.semaphore_wait(barrier, pick([sum(has[d][k] for d in "udyxp") for k in range(depth)]))

    def copy(d, start, count, send, recv):
        piece = held.at[pl.ds(start, count)]
        return pltpu.make_async_remote_copy(
            src_ref=piece, dst_ref=piece, send_sem=send, recv_sem=recv,
            device_id=peers[d], device_id_type=MESH,
        )

    loads[0].wait()
    loads[1].wait()
    for k in range(gathered):
        sub = k + side * special if k < special else special + k
        start = pl.multiple_of(mine + sub * PIECE, PIECE)
        for i, d in enumerate("udy"):
            def send(i=i, d=d, start=start, sub=sub):
                copy(d, start, PIECE, own_sem.at[i], recv_sem.at[pair, sub]).start()
            when(has[d], send)
    copy("p", mine, rows, core_send.at[pair], core_recv.at[pair]).start()

    cols = held.shape[1]
    step = cols // 5 if cols % 5 == 0 else cols

    def multiply(which, fresh):
        copy("p", 0, rows, core_send.at[which], core_recv.at[which]).wait_recv()
        span = pl.ds(pl.multiple_of(which * (2 * rows), 2 * rows), 2 * rows)
        left = tok[:, span]

        @pl.loop(0, cols // step)
        def _(n):
            part = pl.ds(pl.multiple_of(n * step, step), step)
            term = jnp.dot(left, held[span, part], preferred_element_type=jnp.float32)
            acc[:, part] = term if fresh else acc[:, part] + term

    seen = [{} for _ in range(depth)]
    done = [[] for _ in range(depth)]
    total = len(events[0])
    for e in range(total):
        row = [events[k][e] for k in range(depth)]
        owner = pick([r[1] for r in row])
        same = pick([r[2] for r in row])
        offset, slope = [], []
        for r in row:
            if r[0] == "x":
                offset.append(special + r[3])
                slope.append(-special)
            elif r[3] < special:
                offset.append(r[3])
                slope.append(special)
            else:
                offset.append(special + r[3])
                slope.append(0)
        sub = pick(offset) + pick(slope) * side
        which = owner * 2 + (1 - same) + (2 * same - 1) * y
        start = pl.multiple_of((which * 2 + core) * rows + sub * PIECE, PIECE)
        arrived = recv_sem.at[which, sub]
        copy("p", start, PIECE, core_send.at[which], arrived).wait_recv()
        for i, d in enumerate(kinds):
            def relay(i=i, d=d, start=start, which=which, arrived=arrived):
                copy(d, start, PIECE, send_sem.at[i, which], arrived).start()
            when([d in r[4] for r in row], relay)
        copy("p", start, PIECE, core_send.at[which], core_recv.at[which]).start()
        if e == 4:
            loads[2].wait()
            multiply(pair, True)
        for k in range(depth):
            key = row[k][1:3]
            seen[k][key] = seen[k].get(key, 0) + 1
            if seen[k][key] == pieces:
                done[k].append((e, key))
        n = min(len(d) for d in done)
        if n and max(d[n - 1][0] for d in done) == e:
            fresh_done = [m for m in range(n) if max(d[m][0] for d in done) == e]
            for m in fresh_done:
                owners = pick([d[m][1][0] for d in done])
                sames = pick([d[m][1][1] for d in done])
                multiply(owners * 2 + (1 - sames) + (2 * sames - 1) * y, False)

    loads[3].wait()
    tokens = acc.shape[0]
    adapters = scale_ref.shape[0]
    rank = (cols - base_cols) // adapters
    boundary = ((len_ref[0] + (BLOCK - 1)) // BLOCK) * BLOCK
    position = lax.broadcasted_iota(jnp.int32, (tokens, 1), 0)
    second = position >= boundary
    offsets = jnp.where(second, position - boundary, position)
    live = offsets < jnp.where(second, len_ref[1], len_ref[0])
    low = jnp.where(second, ids_ref[1], ids_ref[0]) * rank
    scale = jnp.where(second, scale_ref[ids_ref[1]], scale_ref[ids_ref[0]])
    lane = lax.broadcasted_iota(jnp.int32, (tokens, cols - base_cols), 1)
    chosen = (lane >= low) & (lane < low + rank)
    widened = jnp.where(chosen, acc[:, base_cols:], 0.0).astype(jnp.bfloat16)
    width = base_cols // 3
    for n in range(3):
        part = slice(n * width, (n + 1) * width)
        adapter_out = jnp.dot(widened, up[:, part], preferred_element_type=jnp.float32)
        out_ref[:, part] = jnp.where(live, acc[:, part] + scale * adapter_out, 0.0).astype(out_ref.dtype)

    for i in range(3):
        def sent(i=i):
            copy("udy"[i], 0, gathered * PIECE, own_sem.at[i], recv_sem.at[0, 0]).wait_send()
        when(has["udy"[i]], sent)
    for i, d in enumerate(kinds):
        for owner in range(depth):
            for same in range(2):
                counts = [
                    sum(d in r[4] and r[1:3] == (owner, same) for r in events[k]) for k in range(depth)
                ]
                which = owner * 2 + (1 - same) + (2 * same - 1) * y
                for count in sorted(set(counts) - {0}):
                    def sent(count=count, i=i, d=d, which=which):
                        copy(d, 0, count * PIECE, send_sem.at[i, which], recv_sem.at[0, 0]).wait_send()
                    when([c == count for c in counts], sent)
    for which in range(2 * depth):
        copy("p", 0, rows, core_send.at[which], core_recv.at[which]).wait_send()


def solution(mesh):
    groups, n = mesh.shape["groups"], mesh.shape["dp"]
    depth = n // 4
    swap = groups % 2 == 0

    def local(tokens, base_weight, down_stack, up_stack, adapter_scale, lengths, adapter_ids):
        rows, base_cols = base_weight.shape
        cols = base_cols + down_stack.shape[1]
        pieces = rows // PIECE
        special = (5 * pieces) // 16 if swap else 0
        gathered = pieces - special
        first = tuple(range(gathered - pieces // 8, gathered))
        slots = 2 * depth
        any_space = pl.BlockSpec(memory_space=pl.ANY)
        scalars = pl.BlockSpec(memory_space=pltpu.SMEM)
        return pl.pallas_call(
            functools.partial(kernel, (depth, special, first, swap)),
            out_shape=jax.ShapeDtypeStruct((tokens.shape[0], base_cols), jnp.bfloat16),
            in_specs=[any_space] * 4 + [scalars] * 3,
            out_specs=pl.BlockSpec(memory_space=pltpu.VMEM),
            scratch_shapes=[
                pltpu.VMEM((n * rows, cols), jnp.bfloat16),
                pltpu.VMEM(tokens.shape, jnp.bfloat16),
                pltpu.VMEM(up_stack.shape, jnp.bfloat16),
                pltpu.VMEM((tokens.shape[0], cols), jnp.float32),
                pltpu.SemaphoreType.DMA((4,)),
                pltpu.SemaphoreType.DMA((slots, pieces)),
                pltpu.SemaphoreType.DMA((4, slots)),
                pltpu.SemaphoreType.DMA((3,)),
                pltpu.SemaphoreType.DMA((slots,)),
                pltpu.SemaphoreType.DMA((slots,)),
            ],
            compiler_params=pltpu.CompilerParams(
                collective_id=0, has_side_effects=True, vmem_limit_bytes=56 * 1024 * 1024
            ),
        )(tokens, base_weight, down_stack, up_stack, adapter_scale, lengths, adapter_ids)

    in_specs = (
        P(("groups", "dp"), None), P("dp", None), P("dp", None), P(), P(),
        P(("groups", "dp")), P(("groups", "dp")),
    )
    return jax.shard_map(
        local, mesh=mesh, in_specs=in_specs, out_specs=P(("groups", "dp"), None), check_vma=False
    )
```

time: 209 us -> 86.8 us (0.42)
  waiting for transfers between devices: 160 us -> 0 us
  Pallas kernels: 0 us -> 84.7 us
  matrix products: 17.9 us -> 0 us
  between operations: 13.5 us -> 0.01 us
  local copies, waits for them, and re-layouts: 10.8 us -> 1.92 us
  other arithmetic: 6.4 us -> 0 us
    all_gather x2 -> x0, waiting for transfers between devices: 160 us -> none  [the longest x1 88.3 us: local(): w_piece = lax.all_gather(base_weight, 'dp', axis=0, tiled=True)]
    pallas_call x0 -> x1, Pallas kernels: none -> 84.7 us  [local(): pl.pallas_call(functools.partial(kernel, (depth, special, first, swap)),...]
    dot_general x3 -> x0, matrix products: 17.9 us -> none  [the longest x1 9.92 us: local(): jnp.dot(tokens, w_piece, preferred_element_type=jnp.float32)]
    gather x1 -> x0, local copies, waits for them, and re-layouts: 5.9 us -> none  [local(): selected_adapter = jnp.take(down_split, adapter_per_block, axis=1)]
    select_n x4 -> x0, other arithmetic: 3.17 us -> none  [the longest x1 1.23 us: local(): selected_adapter = jnp.take(down_split, adapter_per_block, axis=1)]
    slice x2 -> x0, local copies, waits for them, and re-layouts: 2.73 us -> none  [the longest x1 1.38 us: layout(): is_live = offset < jnp.where(second, lengths[1], lengths[0])]
  transfers between devices with their start and end apart: 2 -> 0, of which waited for: 2 -> 0; matrix products, arithmetic and copies ran while one was open for 10% -> 0% of each run, Pallas kernels for 0% -> 0%
where the time goes in v1:
time: 86.8 us; the launch traced here: 86.6 us
  Pallas kernels  84.7 us (98%)
  local copies, waits for them, and re-layouts  1.92 us (2%)
    pallas_call x1, Pallas kernels, local(): pl.pallas_call(functools.partial(kernel, (depth, special, first, swap)),...  84.7 us
    unnamed x1, local copies, waits for them, and re-layouts  1.92 us

profile of v1, /device:TPU:0, one launch (start us, length us, event | category | flops | bytes accessed | tf_op | source)
XLA Modules:
  0.0 86.6 jit_solution(3358724476022426726)
XLA Ops:
  0.0 84.7 %shard_map.73 = bf16[384,768]{1,0:T(8,128)(2,1)} custom-call(bf16[384,8192]{1,0:T(8,128)(2,1)} %tok_hbm.1, bf16[512,768]{1,0:T(8,128)(2,1)} %base_hbm.1, bf16[512,512]{1,0:T(8,128)(2,1)} %down_hbm.1, bf16[512,768]{1,0:T(8,128)(2,1)} %up_hbm.1, f32[8]{0:T(128)} %scale_ref.1, s32[2]{0:T(128)} %len_ref.1, s32[2]{0:T(128)} %ids_ref.1), custom_call_target="tpu_custom_call" | custom-call | tf_op jit(solution)/shard_map/pallas_call | solution.py:248
  84.7 1.9 %copy.9 = bf16[384,768]{1,0:T(8,128)(2,1)} copy(bf16[384,768]{1,0:T(8,128)(2,1)} %shard_map.73) | data formatting | bytes 1179648

commit v2 on v1

--- a/solution.py
+++ b/solution.py
@@ -131,24 +131,56 @@
             def send(i=i, d=d, start=start, sub=sub):
                 copy(d, start, PIECE, own_sem.at[i], recv_sem.at[pair, sub]).start()
             when(has[d], send)
-    copy("p", mine, rows, core_send.at[pair], core_recv.at[pair]).start()
+    blocks = core_recv.shape[1]
+    deep = rows // blocks
+    per_block = pieces // blocks
+    for b in range(blocks):
+        copy("p", pl.multiple_of(mine + b * deep, deep), deep, core_send.at[pair], core_recv.at[pair, b]).start()
 
     cols = held.shape[1]
     step = cols // 5 if cols % 5 == 0 else cols
 
-    def multiply(which, fresh):
-        copy("p", 0, rows, core_send.at[which], core_recv.at[which]).wait_recv()
-        span = pl.ds(pl.multiple_of(which * (2 * rows), 2 * rows), 2 * rows)
-        left = tok[:, span]
+    def multiply(which, block, fresh):
+        copy("p", 0, deep, core_send.at[which], core_recv.at[which, block]).wait_recv()
+        spans = [
+            pl.ds(pl.multiple_of((which * 2 + c) * rows + block * deep, deep), deep) for c in range(2)
+        ]
+        left = jnp.concatenate([tok[:, span] for span in spans], axis=1)
 
         @pl.loop(0, cols // step)
         def _(n):
             part = pl.ds(pl.multiple_of(n * step, step), step)
-            term = jnp.dot(left, held[span, part], preferred_element_type=jnp.float32)
+            right = jnp.concatenate([held[span, part] for span in spans], axis=0)
+            term = jnp.dot(left, right, preferred_element_type=jnp.float32)
             acc[:, part] = term if fresh else acc[:, part] + term
 
-    seen = [{} for _ in range(depth)]
-    done = [[] for _ in range(depth)]
+    def landed(side_of):
+        order = []
+        for row in events:
+            seen, found = {}, []
+            for e, (via, owner, same, k, _) in enumerate(row):
+                if via == "x":
+                    sub = (1 - side_of) * special + k
+                else:
+                    sub = side_of * special + k if k < special else special + k
+                key = (owner, same, sub // per_block)
+                seen[key] = seen.get(key, 0) + 1
+                if seen[key] == per_block:
+                    found.append((e, key))
+            order.append(found)
+        return order
+
+    both = [landed(0), landed(1)]
+    ready = []
+    for k in range(depth):
+        last = {}
+        for found in (both[0][k], both[1][k]):
+            for e, key in found:
+                last[key] = max(last.get(key, 0), e)
+        ready.append(sorted((e, key) for key, e in last.items()))
+    due = {}
+    for m in range(len(ready[0])):
+        due.setdefault(max(r[m][0] for r in ready), []).append([r[m][1] for r in ready])
     total = len(events[0])
     for e in range(total):
         row = [events[k][e] for k in range(depth)]
@@ -174,22 +206,15 @@
             def relay(i=i, d=d, start=start, which=which, arrived=arrived):
                 copy(d, start, PIECE, send_sem.at[i, which], arrived).start()
             when([d in r[4] for r in row], relay)
-        copy("p", start, PIECE, core_send.at[which], core_recv.at[which]).start()
+        block = sub // per_block if blocks > 1 else 0
+        copy("p", start, PIECE, core_send.at[which], core_recv.at[which, block]).start()
         if e == 4:
             loads[2].wait()
-            multiply(pair, True)
-        for k in range(depth):
-            key = row[k][1:3]
-            seen[k][key] = seen[k].get(key, 0) + 1
-            if seen[k][key] == pieces:
-                done[k].append((e, key))
-        n = min(len(d) for d in done)
-        if n and max(d[n - 1][0] for d in done) == e:
-            fresh_done = [m for m in range(n) if max(d[m][0] for d in done) == e]
-            for m in fresh_done:
-                owners = pick([d[m][1][0] for d in done])
-                sames = pick([d[m][1][1] for d in done])
-                multiply(owners * 2 + (1 - sames) + (2 * sames - 1) * y, False)
+            for b in range(blocks):
+                multiply(pair, b, b == 0)
+        for keys in due.get(e, []):
+            owners, sames = pick([key[0] for key in keys]), pick([key[1] for key in keys])
+            multiply(owners * 2 + (1 - sames) + (2 * sames - 1) * y, pick([key[2] for key in keys]), False)
 
     loads[3].wait()
     tokens = acc.shape[0]
@@ -227,7 +252,7 @@
                         copy(d, 0, count * PIECE, send_sem.at[i, which], recv_sem.at[0, 0]).wait_send()
                     when([c == count for c in counts], sent)
     for which in range(2 * depth):
-        copy("p", 0, rows, core_send.at[which], core_recv.at[which]).wait_send()
+        copy("p", 0, rows, core_send.at[which], core_recv.at[which, 0]).wait_send()
 
 
 def solution(mesh):
@@ -259,7 +284,7 @@
                 pltpu.SemaphoreType.DMA((slots, pieces)),
                 pltpu.SemaphoreType.DMA((4, slots)),
                 pltpu.SemaphoreType.DMA((3,)),
-                pltpu.SemaphoreType.DMA((slots,)),
+                pltpu.SemaphoreType.DMA((slots, max(1, rows // 256))),
                 pltpu.SemaphoreType.DMA((slots,)),
             ],
             compiler_params=pltpu.CompilerParams(

time: 86.8 us -> 88.2 us (1.016)
  no operation moved by 1% of the time
where the time goes in v2:
time: 88.2 us; the launch traced here: 87.1 us
  Pallas kernels  85.2 us (97%)
  local copies, waits for them, and re-layouts  1.92 us (2%)
    pallas_call x1, Pallas kernels, local(): pl.pallas_call(functools.partial(kernel, (depth, special, first, swap)),...  85.2 us
    unnamed x1, local copies, waits for them, and re-layouts  1.92 us

profile of v2, /device:TPU:0, one launch (start us, length us, event | category | flops | bytes accessed | tf_op | source)
XLA Modules:
  0.0 87.1 jit_solution(5041490409192996017)
XLA Ops:
  0.0 85.2 %shard_map.73 = bf16[384,768]{1,0:T(8,128)(2,1)} custom-call(bf16[384,8192]{1,0:T(8,128)(2,1)} %tok_hbm.1, bf16[512,768]{1,0:T(8,128)(2,1)} %base_hbm.1, bf16[512,512]{1,0:T(8,128)(2,1)} %down_hbm.1, bf16[512,768]{1,0:T(8,128)(2,1)} %up_hbm.1, f32[8]{0:T(128)} %scale_ref.1, s32[2]{0:T(128)} %len_ref.1, s32[2]{0:T(128)} %ids_ref.1), custom_call_target="tpu_custom_call" | custom-call | tf_op jit(solution)/shard_map/pallas_call | solution.py:273
  85.2 1.9 %copy.9 = bf16[384,768]{1,0:T(8,128)(2,1)} copy(bf16[384,768]{1,0:T(8,128)(2,1)} %shard_map.73) | data formatting | bytes 1179648

commit v3 on v2

--- a/solution.py
+++ b/solution.py
@@ -138,21 +138,15 @@
         copy("p", pl.multiple_of(mine + b * deep, deep), deep, core_send.at[pair], core_recv.at[pair, b]).start()
 
     cols = held.shape[1]
-    step = cols // 5 if cols % 5 == 0 else cols
 
     def multiply(which, block, fresh):
         copy("p", 0, deep, core_send.at[which], core_recv.at[which, block]).wait_recv()
         spans = [
             pl.ds(pl.multiple_of((which * 2 + c) * rows + block * deep, deep), deep) for c in range(2)
         ]
-        left = jnp.concatenate([tok[:, span] for span in spans], axis=1)
-
-        @pl.loop(0, cols // step)
-        def _(n):
-            part = pl.ds(pl.multiple_of(n * step, step), step)
-            right = jnp.concatenate([held[span, part] for span in spans], axis=0)
-            term = jnp.dot(left, right, preferred_element_type=jnp.float32)
-            acc[:, part] = term if fresh else acc[:, part] + term
+
+        term = sum(jnp.dot(tok[:, span], held[span, :], preferred_element_type=jnp.float32) for span in spans)
+        acc[...] = term if fresh else acc[...] + term
 
     def landed(side_of):
         order = []

time: 88.2 us -> 82.5 us (0.935); the launches traced: 87.1 us -> 82.3 us
  Pallas kernels: 85.2 us -> 80.4 us
    pallas_call x1, Pallas kernels: 85.2 us -> 80.4 us  [local(): pl.pallas_call(functools.partial(kernel, (depth, special, first, swap)),...]
where the time goes in v3:
time: 82.5 us; the launch traced here: 82.3 us
  Pallas kernels  80.4 us (97%)
  local copies, waits for them, and re-layouts  1.92 us (2%)
    pallas_call x1, Pallas kernels, local(): pl.pallas_call(functools.partial(kernel, (depth, special, first, swap)),...  80.4 us
    unnamed x1, local copies, waits for them, and re-layouts  1.92 us

profile of v3, /device:TPU:0, one launch (start us, length us, event | category | flops | bytes accessed | tf_op | source)
XLA Modules:
  0.0 82.3 jit_solution(8330762829765978560)
XLA Ops:
  0.0 80.4 %shard_map.73 = bf16[384,768]{1,0:T(8,128)(2,1)} custom-call(bf16[384,8192]{1,0:T(8,128)(2,1)} %tok_hbm.1, bf16[512,768]{1,0:T(8,128)(2,1)} %base_hbm.1, bf16[512,512]{1,0:T(8,128)(2,1)} %down_hbm.1, bf16[512,768]{1,0:T(8,128)(2,1)} %up_hbm.1, f32[8]{0:T(128)} %scale_ref.1, s32[2]{0:T(128)} %len_ref.1, s32[2]{0:T(128)} %ids_ref.1), custom_call_target="tpu_custom_call" | custom-call | tf_op jit(solution)/shard_map/pallas_call | solution.py:267
  80.4 1.9 %copy.9 = bf16[384,768]{1,0:T(8,128)(2,1)} copy(bf16[384,768]{1,0:T(8,128)(2,1)} %shard_map.73) | data formatting | bytes 1179648
